TPU v7x, 32 devices: a whole 2x2x4 slice. The times are simulated.
32 devices in a mesh: wide: 2 (over x), narrow: 4 (over y, core), seq: 4 (over z).
Axes of the slice: x: 2, y: 2, z: 4, core: 2. Of those that a mesh axis runs over, the one named last changes fastest.
Arguments:
- attn_query: bfloat16 [1024, 73728], P(('seq', 'wide'), 'narrow'), parts along dimension 0, may hold values from -6 to 6
- key_latent: bfloat16 [1024, 576], P(('seq', 'wide')), parts along dimension 0, may hold values from -6 to 6
- lse_attn: float32 [128, 1024], P('narrow', ('seq', 'wide')), parts along dimension 1, may hold values from 1 to 3
- index_query: bfloat16 [1024, 8192], P(('seq', 'wide'), 'narrow'), parts along dimension 0, may hold values from -6 to 6
- index_key: bfloat16 [1024, 128], P(('seq', 'wide')), parts along dimension 0, may hold values from -6 to 6
- index_weight: float32 [64, 1024], P('narrow', ('seq', 'wide')), parts along dimension 1, may hold values from -0.75 to 0.75
- lse_index: float32 [1024], P(('seq', 'wide')), parts along dimension 0, may hold values from 0 to 1
- block_order: int32 [8], P('seq'), parts along dimension 0, may hold values from 0 to 127, as said below
Outputs:
- d_index_query: float32 [1024, 8192], P(('seq', 'wide'), 'narrow'), parts along dimension 0
- d_index_weight: float32 [64, 1024], P('narrow', ('seq', 'wide')), parts along dimension 1
- d_index_key: float32 [1024, 128], P(('seq', 'wide')), parts along dimension 0
There are 4 independent parts, one for each index of `seq`. A program takes and returns all parts, laid end to end along the dimension named above; each array names one. Nothing has to cross between parts.
Inputs may be any that keep to these rules, and one draw needn't show every extreme that they name: Index d of wide holds tokens 128 * block_order[d] to 128 * block_order[d] + 127 of the context; the values are distinct.
All inputs are finite; a program needn't handle non-finite values.
Results may differ from a plain program's by a relative error of at most 0.008.
Values may be sent and summed in bfloat16 or wider, within the bound.
No kernel may reach another device: no remote copies, remote signals or barrier semaphores. Data moves between devices by JAX's collectives and lax.ppermute only.
A program may use at most 64 MiB of HBM per device.

v0:
```python
import jax
import jax.numpy as jnp
from jax import lax
from jax.sharding import PartitionSpec as P

HEADS = 128
attn_scale = 192.0 ** (-0.5)


def shifted(block, axis, distance):
    devices = range(lax.axis_size(axis))
    route = [((i - distance) % len(devices), i) for i in devices]
    return lax.ppermute(block, axis, route)


def body(
    attn_query, key_latent, lse_attn, index_query, index_key, index_weight, lse_index, block_order
):
    tok_rows = key_latent.shape[0]
    key_width = key_latent.shape[1]
    index_width = index_key.shape[1]
    heads_here = attn_query.shape[1] // key_width
    iheads_here = index_query.shape[1] // index_width
    cycle_size = lax.axis_size("wide")
    cycle_place = lax.axis_index("wide")
    query_heads = attn_query.reshape(tok_rows, heads_here, key_width)
    index_heads = index_query.reshape(tok_rows, iheads_here, index_width)
    offsets = jnp.arange(tok_rows, dtype=jnp.int32)
    query_pos = block_order[cycle_place] * tok_rows + offsets
    lse_rows = jnp.transpose(lse_attn)
    weight_rows = jnp.transpose(index_weight)
    index_scale = index_width ** (-0.5)

    def block_grads(key_block, ikey_block, source):
        key_pos = block_order[source] * tok_rows + offsets
        causal = query_pos[:, None] >= key_pos[None, :]
        scores = (
            jnp.einsum("thc,sc->ths", query_heads, key_block, preferred_element_type=jnp.float32)
            * attn_scale
        )
        part_target = jnp.sum(jnp.exp(scores - lse_rows[:, :, None]), axis=1) / HEADS
        logits = (
            jnp.einsum("tjc,sc->tjs", index_heads, ikey_block, preferred_element_type=jnp.float32)
            * index_scale
        )
        active = jnp.maximum(logits, 0.0)
        part_score = jnp.einsum("tjs,tj->ts", active, weight_rows)
        target, score = lax.psum((part_target, part_score), "narrow")
        difference = jnp.where(causal, jnp.exp(score - lse_index[:, None]) - target, 0.0)
        grad_weight = jnp.einsum("ts,tjs->tj", difference, active)
        coefficient = (
            difference[:, None, :]
            * weight_rows[:, :, None]
            * (logits > 0.0).astype(jnp.float32)
            * index_scale
        ).astype(jnp.bfloat16)
        grad_query = jnp.einsum(
            "tjs,sc->tjc", coefficient, ikey_block, preferred_element_type=jnp.float32
        )
        grad_key = jnp.einsum(
            "tjs,tjc->sc", coefficient, index_heads, preferred_element_type=jnp.float32
        )
        return (grad_query, grad_weight, grad_key)

    def move_keys(key_block, ikey_block):
        return shifted((key_block, ikey_block), "wide", 1)

    zero_query = jnp.zeros((tok_rows, iheads_here, index_width), jnp.float32)
    zero_weight = jnp.zeros((tok_rows, iheads_here), jnp.float32)
    last_source = (cycle_place + 1) % cycle_size

    def pass_grad(carried):
        return shifted(carried, "wide", 1)

    def cycle_step(step_index, carried_state):
        key_block, ikey_block, carried, sum_query, sum_weight = carried_state
        source = (cycle_place - step_index) % cycle_size
        grad_query, grad_weight, grad_key = block_grads(key_block, ikey_block, source)
        key_block, ikey_block = move_keys(key_block, ikey_block)
        return (
            key_block,
            ikey_block,
            pass_grad(carried + grad_key),
            sum_query + grad_query,
            sum_weight + grad_weight,
        )

    start_state = (
        key_latent,
        index_key,
        jnp.zeros((tok_rows, index_width), jnp.float32),
        zero_query,
        zero_weight,
    )
    key_block, ikey_block, carried, sum_query, sum_weight = lax.fori_loop(
        0, cycle_size - 1, cycle_step, start_state
    )
    grad_query, grad_weight, grad_key = block_grads(key_block, ikey_block, last_source)
    own_key = pass_grad(carried + grad_key)
    key_total = lax.psum(own_key, "narrow")
    sum_query = sum_query + grad_query
    sum_weight = sum_weight + grad_weight
    return (
        sum_query.reshape(tok_rows, iheads_here * index_width),
        jnp.transpose(sum_weight),
        key_total,
    )


def solution(mesh):
    in_specs = (
        P(("seq", "wide"), "narrow"),
        P(("seq", "wide"), None),
        P("narrow", ("seq", "wide")),
        P(("seq", "wide"), "narrow"),
        P(("seq", "wide"), None),
        P("narrow", ("seq", "wide")),
        P(("seq", "wide")),
        P("seq"),
    )
    out_specs = (
        P(("seq", "wide"), "narrow"),
        P("narrow", ("seq", "wide")),
        P(("seq", "wide"), None),
    )
    return jax.shard_map(body, mesh=mesh, in_specs=in_specs, out_specs=out_specs, check_vma=False)
```

profile of v0, /device:TPU:0, one launch (start us, length us, event | category | flops | bytes accessed | tf_op | source)
XLA Modules:
  0.0 119.6 jit_solution(2977630586859763670)
XLA Ops:
  7.2 0.0 copy-start
  7.2 0.0 all-reduce.6.cloned.1.call-start
  7.2 3.0 %collective-permute-start = (bf16[128,128]{1,0:T(8,128)(2,1)}, bf16[128,128]{1,0:T(8,128)(2,1)S(1)}, u32[]{:S(2)}, u32[]{:S(2)}) collective-permute-start(bf16[128,128]{1,0:T(8,128)(2,1)} %param.12), channel_id=1, source_target_pairs={{16,0},{0,16},{17,1},{1,17},{18,2},{2,18},{19,3},{3,19},{20,4},{4,... | collective-permute-start | bytes 98312 | tf_op jit(solution)/shard_map/while/body/eval_jaxpr/ppermute | solution.py:13
  10.3 0.1 collective-permute-start.1
  10.3 1.4 %fusion.43 = (s32[1]{0:T(128)}, s32[1]{0:T(128)}, s32[1]{0:T(128)}) fusion(s32[2]{0:T(128)} %param.15, s32[]{:T(128)S(6)} %select_n.36, s32[]{:T(128)S(6)} %select_n.31, s32[]{:T(128)S(6)} %select_n.33), kind=kLoop, calls=%fused_computation.67 | loop fusion | bytes 36 | tf_op jit(solution)/shard_map/dynamic_slice | solution.py:35
  13.6 0.8 copy.33
  14.5 0.0 copy-done
  14.5 1.1 broadcast_maximum_fusion.1
  15.6 0.1 fusion.9
  15.7 0.0 copy-start.5
  15.7 0.0 copy-start.6
  15.7 6.7 %copy.23 = bf16[128,18432]{0,1:T(8,128)(2,1)} copy(bf16[128,18432]{1,0:T(8,128)(2,1)} %param.8) | data formatting | bytes 9437184 | tf_op args[0]
  22.4 0.0 slice-start
  22.4 0.0 copy-done.5
  22.4 0.0 copy-done.6
  22.4 0.0 slice-start.1
  22.4 4.5 %exponential_reduce_fusion.1 = f32[128,128]{1,0:T(8,128)S(1)} fusion(bf16[128,32,576]{0,2,1:T(8,128)(2,1)} %bitcast.87, f32[128,32]{0,1:T(8,128)S(1)} %bitcast.101, bf16[128,576]{0,1:T(8,128)(2,1)S(1)} %copy-done.5), kind=kOutput, calls=%fused_computation.1 | convolution fusion | flops 605536256 | bytes 4947968 | tf_op jit(solution)/shard_map/while/body/eval_jaxpr/thc,sc->ths/dot_general | solution.py:38
  26.9 0.6 broadcast_multiply_fusion.1
  27.6 1.1 fusion.7
  28.6 0.0 collective-permute-done
  28.6 0.3 broadcast_maximum_fusion
  29.0 1.1 fusion.3
  30.0 0.0 copy-start.4
  30.0 0.0 copy-start.3
  30.0 0.0 collective-permute-done.1
  30.0 0.0 slice-done
  30.0 0.0 slice-done.1
  30.0 2.2 %exponential_reduce_fusion = f32[128,128]{1,0:T(8,128)S(1)} fusion(bf16[128,32,576]{0,2,1:T(8,128)(2,1)S(1)} %bitcast.90, f32[128,32]{0,1:T(8,128)S(1)} %bitcast.102, bf16[128,576]{0,1:T(8,128)(2,1)S(1)} %collective-permute-done.1), kind=kOutput, calls=%fused_computation | convolution fusion | flops 605536256 | bytes 4947968 | tf_op jit(solution)/shard_map/thc,sc->ths/dot_general | solution.py:38
  32.2 0.6 broadcast_multiply_fusion
  32.8 0.0 all-reduce.6.cloned.1.call-update
  32.9 0.0 all-reduce.4.cloned.1.call-start
  32.9 0.0 copy-start.2
  32.9 0.1 fusion.10
  33.1 34.1 %all-reduce.6.cloned.1.call-done = (f32[128,128]{1,0:T(8,128)}, f32[128,128]{1,0:T(8,128)}, f32[128,128]{1,0:T(8,128)}, f32[128,128]{1,0:T(8,128)}) async-done(((f32[128,128]{1,0:T(8,128)}, f32[128,128]{1,0:T(8,128)}, f32[128,128]{1,0:T(8,128)}, f32[128,128]{1,0:T(8,128)}), (f32[128,128]{1,0:T(8,128)}, f32[128,128]{1,0:T(8,128)}, f32[128,128]{1,0:T(8,128)}, ...) | async-done | bytes 262160 | tf_op jit(solution)/shard_map/while/body/eval_jaxpr/psum | solution.py:48
  67.2 0.0 copy-done.4
  67.2 1.0 subtract_select_fusion
  68.3 0.0 copy-done.3
  68.3 0.7 convolution_bitcast_fusion.1
  69.0 0.0 copy-done.2
  69.0 0.6 fusion.15
  69.6 1.5 %collective-permute-start.2 = (f32[128,128]{1,0:T(8,128)S(1)}, f32[128,128]{1,0:T(8,128)S(1)}, u32[]{:S(2)}, u32[]{:S(2)}) collective-permute-start(f32[128,128]{1,0:T(8,128)S(1)} %convolution_bitcast_fusion.1), channel_id=1, source_target_pairs={{16,0},{0,16},{17,1},{1,17},{18,2},{2,18},{19,3},{3,19},{20,4},{4,... | collective-permute-start | bytes 196616 | tf_op jit(solution)/shard_map/while/body/eval_jaxpr/ppermute | solution.py:13
  71.1 0.6 convolution_add_fusion
  71.7 0.4 fusion.1
  72.1 1.8 %collective-permute-done.2 = f32[128,128]{1,0:T(8,128)S(1)} collective-permute-done((f32[128,128]{1,0:T(8,128)S(1)}, f32[128,128]{1,0:T(8,128)S(1)}, u32[]{:S(2)}, u32[]{:S(2)}) %collective-permute-start.2) | collective-permute-done | bytes 65568 | tf_op jit(solution)/shard_map/while/body/eval_jaxpr/ppermute | solution.py:13
  73.9 0.7 fusion
  74.6 1.5 %collective-permute-start.3 = (f32[128,128]{1,0:T(8,128)S(1)}, f32[128,128]{1,0:T(8,128)S(1)}, u32[]{:S(2)}, u32[]{:S(2)}) collective-permute-start(f32[128,128]{1,0:T(8,128)S(1)} %fusion), channel_id=1, source_target_pairs={{16,0},{0,16},{17,1},{1,17},{18,2},{2,18},{19,3},{3,19},{20,4},{4,... | collective-permute-start | bytes 196616 | tf_op jit(solution)/shard_map/ppermute | solution.py:13
  76.2 0.4 fusion.5
  76.6 0.1 copy.42
  76.7 0.1 copy.40
  76.7 2.2 %collective-permute-done.3 = f32[128,128]{1,0:T(8,128)S(1)} collective-permute-done((f32[128,128]{1,0:T(8,128)S(1)}, f32[128,128]{1,0:T(8,128)S(1)}, u32[]{:S(2)}, u32[]{:S(2)}) %collective-permute-start.3) | collective-permute-done | bytes 65568 | tf_op jit(solution)/shard_map/ppermute | solution.py:13
  79.0 0.0 copy-start.1
  79.0 0.6 copy-done.1
  79.6 0.0 all-reduce.4.cloned.1.call-update
  79.6 0.6 fusion.30
  80.2 1.3 %copy.31 = f32[128,2048]{1,0:T(8,128)} copy(f32[128,2048]{0,1:T(8,128)S(1)} %bitcast.91) | data formatting | bytes 2097152
  81.5 29.8 %all-reduce.4.cloned.1.call-done = f32[128,128]{1,0:T(8,128)} async-done(((f32[128,128]{1,0:T(8,128)}), f32[128,128]{1,0:T(8,128)}) %all-reduce.4.cloned.1.call-update) | async-done | bytes 65552 | tf_op jit(solution)/shard_map/psum | solution.py:100
  111.3 1.5 %copy.82 = f32[128,128]{1,0:T(8,128)} copy(f32[128,128]{1,0:T(8,128)} %all-reduce.4.cloned.1.call-done) | data formatting | bytes 131072
  (3 shorter events, 0.0 us)
Async XLA Ops:
  7.2 7.3 %copy-start = (bf16[128,2048]{1,0:T(8,128)(2,1)S(1)}, bf16[128,2048]{1,0:T(8,128)(2,1)}, u32[]{:S(2)}) copy-start(bf16[128,2048]{1,0:T(8,128)(2,1)} %param.11) | copy-start | bytes 1572868
  7.2 60.0 %all-reduce.6.cloned.1.call-start = ((), (), s32[]{:S(2)}) async-start(), calls=%async_computation.1 | async-start | bytes 524288 | tf_op jit(solution)/shard_map/while/body/eval_jaxpr/psum | solution.py:48
  7.2 21.4 %collective-permute-start = (bf16[128,128]{1,0:T(8,128)(2,1)}, bf16[128,128]{1,0:T(8,128)(2,1)S(1)}, u32[]{:S(2)}, u32[]{:S(2)}) collective-permute-start(bf16[128,128]{1,0:T(8,128)(2,1)} %param.12), channel_id=1, source_target_pairs={{16,0},{0,16},{17,1},{1,17},{18,2},{2,18},{19,3},{3,19},{20,4},{4,... | collective-permute-start | bytes 98312 | tf_op jit(solution)/shard_map/while/body/eval_jaxpr/ppermute | solution.py:13
  10.3 19.8 %collective-permute-start.1 = (bf16[128,576]{0,1:T(8,128)(2,1)}, bf16[128,576]{0,1:T(8,128)(2,1)S(1)}, u32[]{:S(2)}, u32[]{:S(2)}) collective-permute-start(bf16[128,576]{0,1:T(8,128)(2,1)} %param.9), channel_id=1, source_target_pairs={{16,0},{0,16},{17,1},{1,17},{18,2},{2,18},{19,3},{3,19},{20,4},{4,... | collective-permute-start | bytes 442376 | tf_op jit(solution)/shard_map/while/body/eval_jaxpr/ppermute | solution.py:13
  15.7 6.7 %copy-start.5 = (bf16[128,576]{0,1:T(8,128)(2,1)S(1)}, bf16[128,576]{0,1:T(8,128)(2,1)}, u32[]{:S(2)}) copy-start(bf16[128,576]{0,1:T(8,128)(2,1)} %param.9) | copy-start | bytes 442372
  15.7 6.7 %copy-start.6 = (f32[32,128]{1,0:T(8,128)S(1)}, f32[32,128]{1,0:T(8,128)}, u32[]{:S(2)}) copy-start(f32[32,128]{1,0:T(8,128)} %param.10) | copy-start | bytes 49156
  22.4 7.6 %slice-start = ((s8[4718592]{0:T(1024)(128)(4,1)}), s8[4194304]{0:T(1024)(128)(4,1)S(1)}, s32[]{:S(2)}) async-start(s8[4718592]{0:T(1024)(128)(4,1)} %bitcast.88), calls=%async_computation.2 | async-start | bytes 8388608
  22.4 7.6 %slice-start.1 = ((s8[4718592]{0:T(1024)(128)(4,1)}), s8[524288]{0:T(1024)(128)(4,1)S(1)}, s32[]{:S(2)}) async-start(s8[4718592]{0:T(1024)(128)(4,1)} %bitcast.88), calls=%async_computation.3 | async-start | bytes 1048576
  30.0 37.2 %copy-start.4 = (f32[128]{0:T(128)S(1)}, f32[128]{0:T(128)}, u32[]{:S(2)}) copy-start(f32[128]{0:T(128)} %param.14) | copy-start | bytes 1540
  30.0 38.3 %copy-start.3 = (f32[16,128]{1,0:T(8,128)S(1)}, f32[16,128]{1,0:T(8,128)}, u32[]{:S(2)}) copy-start(f32[16,128]{1,0:T(8,128)} %param.13) | copy-start | bytes 24580
  32.9 78.4 %all-reduce.4.cloned.1.call-start = ((), (), s32[]{:S(2)}) async-start(), calls=%async_computation | async-start | bytes 131072 | tf_op jit(solution)/shard_map/psum | solution.py:100
  32.9 36.1 %copy-start.2 = (bf16[128,128]{1,0:T(8,128)(2,1)S(1)}, bf16[128,128]{1,0:T(8,128)(2,1)}, u32[]{:S(2)}) copy-start(bf16[128,128]{1,0:T(8,128)(2,1)} %param.12) | copy-start | bytes 98308
  69.6 4.3 %collective-permute-start.2 = (f32[128,128]{1,0:T(8,128)S(1)}, f32[128,128]{1,0:T(8,128)S(1)}, u32[]{:S(2)}, u32[]{:S(2)}) collective-permute-start(f32[128,128]{1,0:T(8,128)S(1)} %convolution_bitcast_fusion.1), channel_id=1, source_target_pairs={{16,0},{0,16},{17,1},{1,17},{18,2},{2,18},{19,3},{3,19},{20,4},{4,... | collective-permute-start | bytes 196616 | tf_op jit(solution)/shard_map/while/body/eval_jaxpr/ppermute | solution.py:13
  74.6 4.3 %collective-permute-start.3 = (f32[128,128]{1,0:T(8,128)S(1)}, f32[128,128]{1,0:T(8,128)S(1)}, u32[]{:S(2)}, u32[]{:S(2)}) collective-permute-start(f32[128,128]{1,0:T(8,128)S(1)} %fusion), channel_id=1, source_target_pairs={{16,0},{0,16},{17,1},{1,17},{18,2},{2,18},{19,3},{3,19},{20,4},{4,... | collective-permute-start | bytes 196616 | tf_op jit(solution)/shard_map/ppermute | solution.py:13
  79.0 0.6 copy-start.1
Sparse Core Ops, SparseCore 0:
  33.0 34.1 all-reduce.5
  79.7 31.5 all-reduce.3
where the time goes:
time: 120 us
  waiting for transfers between devices  67.9 us (57%)
  between operations  16.2 us (14%)
  matrix products  13.6 us (11%)
  local copies, waits for them, and re-layouts  12.4 us (10%)
  starting transfers between devices  6.27 us (5%)
  other arithmetic  3.2 us (3%)
    psum x1, waiting for transfers between devices, block_grads(): target, score = lax.psum((part_target, part_score), 'narrow')  34.1 us
    psum x1, waiting for transfers between devices, body(): key_total = lax.psum(own_key, 'narrow')  29.8 us
    unnamed x21, local copies, waits for them, and re-layouts  10.1 us
    dot_general x2, matrix products, block_grads(): jnp.einsum('thc,sc->ths', query_heads, key_block, preferred_element_type=...  6.66 us
    ppermute x4, starting transfers between devices, shifted(): return lax.ppermute(block, axis, route)  6.19 us
    ppermute x4, waiting for transfers between devices, shifted(): return lax.ppermute(block, axis, route)  4 us
  transfers between devices with their start and end apart: 6, of which 4 were waited for; matrix products, arithmetic and copies ran while one was open for 18% of the time, Pallas kernels for 0%

commit v1 on v0

--- a/solution.py
+++ b/solution.py
@@ -97,7 +97,7 @@
     )
     grad_query, grad_weight, grad_key = block_grads(key_block, ikey_block, last_source)
     own_key = pass_grad(carried + grad_key)
-    key_total = lax.psum(own_key, "narrow")
+    key_total = jnp.sum(lax.all_gather(own_key, "narrow"), axis=0)
     sum_query = sum_query + grad_query
     sum_weight = sum_weight + grad_weight
     return (

time: 120 us -> 93.1 us (0.78)
  waiting for transfers between devices: 67.9 us -> 36.8 us
  blocking collectives: 0 us -> 5.76 us
  local copies, waits for them, and re-layouts: 12.4 us -> 10.3 us
    psum x1 -> x0, waiting for transfers between devices: 29.8 us -> none  [body(): key_total = lax.psum(own_key, 'narrow')]
    all_gather x0 -> x1, blocking collectives: none -> 5.76 us  [body(): key_total = jnp.sum(lax.all_gather(own_key, 'narrow'), axis=0)]
    unnamed x21 -> x18, local copies, waits for them, and re-layouts: 10.1 us -> 8.02 us
    ppermute x4, waiting for transfers between devices: 4 us -> 2.54 us  [shifted(): return lax.ppermute(block, axis, route)]
  transfers between devices with their start and end apart: 6 -> 5, of which waited for: 4 -> 3; matrix products, arithmetic and copies ran while one was open for 18% -> 23% of each run, Pallas kernels for 0% -> 0%
where the time goes in v1:
time: 93.1 us; the launch traced here: 92.7 us
  waiting for transfers between devices  36.8 us (40%)
  between operations  16.1 us (17%)
  matrix products  13.6 us (15%)
  local copies, waits for them, and re-layouts  10.3 us (11%)
  starting transfers between devices  6.19 us (7%)
  blocking collectives  5.76 us (6%)
  other arithmetic  3.83 us (4%)
    psum x1, waiting for transfers between devices, block_grads(): target, score = lax.psum((part_target, part_score), 'narrow')  34.2 us
    unnamed x18, local copies, waits for them, and re-layouts  8.02 us
    dot_general x2, matrix products, block_grads(): jnp.einsum('thc,sc->ths', query_heads, key_block, preferred_element_type=...  6.67 us
    ppermute x4, starting transfers between devices, shifted(): return lax.ppermute(block, axis, route)  6.15 us
    all_gather x1, blocking collectives, body(): key_total = jnp.sum(lax.all_gather(own_key, 'narrow'), axis=0)  5.76 us
    ppermute x4, waiting for transfers between devices, shifted(): return lax.ppermute(block, axis, route)  2.54 us
    dot_general x2, matrix products, block_grads(): part_score = jnp.einsum('tjs,tj->ts', active, weight_rows)  2.13 us
  transfers between devices with their start and end apart: 5, of which 3 were waited for; matrix products, arithmetic and copies ran while one was open for 23% of the time, Pallas kernels for 0%

profile of v1, /device:TPU:0, one launch (start us, length us, event | category | flops | bytes accessed | tf_op | source)
XLA Modules:
  0.0 92.7 jit_solution(16701534698627602260)
XLA Ops:
  7.2 0.0 copy-start
  7.2 0.0 all-reduce.3.cloned.1.call-start
  7.2 3.0 %collective-permute-start = (bf16[128,128]{1,0:T(8,128)(2,1)}, bf16[128,128]{1,0:T(8,128)(2,1)S(1)}, u32[]{:S(2)}, u32[]{:S(2)}) collective-permute-start(bf16[128,128]{1,0:T(8,128)(2,1)} %param.12), channel_id=1, source_target_pairs={{16,0},{0,16},{17,1},{1,17},{18,2},{2,18},{19,3},{3,19},{20,4},{4,... | collective-permute-start | bytes 98312 | tf_op jit(solution)/shard_map/while/body/eval_jaxpr/ppermute | solution.py:13
  10.3 0.1 collective-permute-start.1
  10.3 1.4 %fusion.43 = (s32[1]{0:T(128)}, s32[1]{0:T(128)}, s32[1]{0:T(128)}) fusion(s32[2]{0:T(128)} %param.15, s32[]{:T(128)S(6)} %select_n.36, s32[]{:T(128)S(6)} %select_n.31, s32[]{:T(128)S(6)} %select_n.33), kind=kLoop, calls=%fused_computation.67 | loop fusion | bytes 36 | tf_op jit(solution)/shard_map/dynamic_slice | solution.py:35
  13.6 0.8 copy.33
  14.5 0.0 copy-done
  14.5 1.1 %broadcast_maximum_fusion.1 = (bf16[128,16,128]{2,0,1:T(8,128)(2,1)S(1)}, f32[128,16,128]{2,0,1:T(8,128)S(1)}) fusion(bf16[128,128]{1,0:T(8,128)(2,1)} %param.12, bf16[128,2048]{1,0:T(8,128)(2,1)S(1)} %copy-done), kind=kOutput, calls=%fused_computation.30 | convolution fusion | flops 67895296 | bytes 2129920 | tf_op jit(solution)/shard_map/while/body/eval_jaxpr/tjc,sc->tjs/dot_general | solution.py:43
  15.6 0.1 fusion.9
  15.7 0.0 copy-start.4
  15.7 0.0 copy-start.5
  15.7 6.7 %copy.23 = bf16[128,18432]{0,1:T(8,128)(2,1)} copy(bf16[128,18432]{1,0:T(8,128)(2,1)} %param.8) | data formatting | bytes 9437184 | tf_op args[0]
  22.4 0.0 slice-start
  22.4 0.0 copy-done.4
  22.4 0.0 copy-done.5
  22.4 0.0 slice-start.1
  22.4 4.5 %exponential_reduce_fusion.1 = f32[128,128]{1,0:T(8,128)S(1)} fusion(bf16[128,32,576]{0,2,1:T(8,128)(2,1)} %bitcast.88, f32[128,32]{0,1:T(8,128)S(1)} %bitcast.103, bf16[128,576]{0,1:T(8,128)(2,1)S(1)} %copy-done.4), kind=kOutput, calls=%fused_computation.1 | convolution fusion | flops 605536256 | bytes 4947968 | tf_op jit(solution)/shard_map/while/body/eval_jaxpr/thc,sc->ths/dot_general | solution.py:38
  26.9 0.6 broadcast_multiply_fusion.1
  27.6 1.1 %fusion.7 = f32[128,1,128]{2,1,0:T(1,128)} fusion(bf16[128,16,1]{1,2,0:T(2,128)(2,1)S(1)} %copy.33, bf16[128,16,128]{2,0,1:T(8,128)(2,1)S(1)} %get-tuple-element.66), kind=kOutput, calls=%fused_computation.21 | convolution fusion | flops 524288 | bytes 593920 | tf_op jit(solution)/shard_map/while/body/eval_jaxpr/tjs,tj->ts/dot_general | solution.py:47
  28.6 0.0 collective-permute-done
  28.6 0.3 broadcast_maximum_fusion
  29.0 1.1 %fusion.3 = f32[128,1,128]{2,1,0:T(1,128)} fusion(bf16[128,16,1]{1,2,0:T(2,128)(2,1)S(1)} %copy.33, bf16[128,16,128]{2,0,1:T(8,128)(2,1)S(1)} %get-tuple-element.68), kind=kOutput, calls=%fused_computation.17 | convolution fusion | flops 524288 | bytes 593920 | tf_op jit(solution)/shard_map/tjs,tj->ts/dot_general | solution.py:47
  30.0 0.0 copy-start.3
  30.0 0.0 copy-start.2
  30.0 0.0 collective-permute-done.1
  30.0 0.0 slice-done
  30.1 0.0 slice-done.1
  30.1 2.2 %exponential_reduce_fusion = f32[128,128]{1,0:T(8,128)S(1)} fusion(bf16[128,32,576]{0,2,1:T(8,128)(2,1)S(1)} %bitcast.91, f32[128,32]{0,1:T(8,128)S(1)} %bitcast.104, bf16[128,576]{0,1:T(8,128)(2,1)S(1)} %collective-permute-done.1), kind=kOutput, calls=%fused_computation | convolution fusion | flops 605536256 | bytes 4947968 | tf_op jit(solution)/shard_map/thc,sc->ths/dot_general | solution.py:38
  32.2 0.6 broadcast_multiply_fusion
  32.9 0.0 all-reduce.3.cloned.1.call-update
  32.9 0.0 copy-start.1
  32.9 0.1 fusion.10
  33.1 34.2 %all-reduce.3.cloned.1.call-done = (f32[128,128]{1,0:T(8,128)}, f32[128,128]{1,0:T(8,128)}, f32[128,128]{1,0:T(8,128)}, f32[128,128]{1,0:T(8,128)}) async-done(((f32[128,128]{1,0:T(8,128)}, f32[128,128]{1,0:T(8,128)}, f32[128,128]{1,0:T(8,128)}, f32[128,128]{1,0:T(8,128)}), (f32[128,128]{1,0:T(8,128)}, f32[128,128]{1,0:T(8,128)}, f32[128,128]{1,0:T(8,128)}, ...) | async-done | bytes 262160 | tf_op jit(solution)/shard_map/while/body/eval_jaxpr/psum | solution.py:48
  67.3 0.0 copy-done.3
  67.3 1.0 %subtract_select_fusion = (f32[128,128]{1,0:T(8,128)S(1)}, f32[128,128]{1,0:T(8,128)S(1)}) fusion(f32[128,128]{1,0:T(8,128)} %get-tuple-element.43, f32[128,128]{1,0:T(8,128)} %get-tuple-element.44, s32[128]{0:T(128)S(1)} %get-tuple-element.70, f32[128]{0:T(128)S(1)} %copy-done.3, s32[128]{0:T(128)S(1)} %iota_add_fusion.2, f32[128,128]{1,0:T(8,128)} %get-tuple-element.41, ...), kind=kLoop, calls=%fused_computation.42 | loop fusion | flops 131072 | bytes 395264 | tf_op jit(solution)/shard_map/jit(_where)/select_n | solution.py:49
  68.3 0.0 copy-done.2
  68.3 0.7 convolution_bitcast_fusion.1
  69.0 0.0 copy-done.1
  69.0 0.6 fusion.15
  69.6 0.4 fusion.1
  70.0 1.5 %collective-permute-start.2 = (f32[128,128]{1,0:T(8,128)S(1)}, f32[128,128]{1,0:T(8,128)S(1)}, u32[]{:S(2)}, u32[]{:S(2)}) collective-permute-start(f32[128,128]{1,0:T(8,128)S(1)} %convolution_bitcast_fusion.1), channel_id=1, source_target_pairs={{16,0},{0,16},{17,1},{1,17},{18,2},{2,18},{19,3},{3,19},{20,4},{4,... | collective-permute-start | bytes 196616 | tf_op jit(solution)/shard_map/while/body/eval_jaxpr/ppermute | solution.py:13
  71.6 0.6 convolution_add_fusion
  72.2 0.4 fusion.5
  72.6 0.1 copy.42
  72.6 0.1 copy.40
  72.7 1.6 %collective-permute-done.2 = f32[128,128]{1,0:T(8,128)S(1)} collective-permute-done((f32[128,128]{1,0:T(8,128)S(1)}, f32[128,128]{1,0:T(8,128)S(1)}, u32[]{:S(2)}, u32[]{:S(2)}) %collective-permute-start.2) | collective-permute-done | bytes 65568 | tf_op jit(solution)/shard_map/while/body/eval_jaxpr/ppermute | solution.py:13
  74.4 0.7 fusion
  75.1 1.5 %collective-permute-start.3 = (f32[128,128]{1,0:T(8,128)S(1)}, f32[128,128]{1,0:T(8,128)S(1)}, u32[]{:S(2)}, u32[]{:S(2)}) collective-permute-start(f32[128,128]{1,0:T(8,128)S(1)} %fusion), channel_id=1, source_target_pairs={{16,0},{0,16},{17,1},{1,17},{18,2},{2,18},{19,3},{3,19},{20,4},{4,... | collective-permute-start | bytes 196616 | tf_op jit(solution)/shard_map/ppermute | solution.py:13
  76.6 0.6 fusion.30
  77.2 1.3 %copy.31 = f32[128,2048]{1,0:T(8,128)} copy(f32[128,2048]{0,1:T(8,128)S(1)} %bitcast.93) | data formatting | bytes 2097152
  78.5 0.9 collective-permute-done.3
  79.4 5.8 %all-gather = f32[512,128]{1,0:T(8,128)S(1)} all-gather(f32[128,128]{1,0:T(8,128)S(1)} %collective-permute-done.3), channel_id=2, replica_groups=mesh['wide'=2,'narrow'=4,'seq'=4] {'narrow'}, dimensions={0}, use_global_device_ids=true | all-gather | bytes 327680 | tf_op jit(solution)/shard_map/all_gather | solution.py:100
  85.2 0.6 reduce_sum.30
  (3 shorter events, 0.0 us)
Async XLA Ops:
  7.2 7.3 %copy-start = (bf16[128,2048]{1,0:T(8,128)(2,1)S(1)}, bf16[128,2048]{1,0:T(8,128)(2,1)}, u32[]{:S(2)}) copy-start(bf16[128,2048]{1,0:T(8,128)(2,1)} %param.11) | copy-start | bytes 1572868
  7.2 60.1 %all-reduce.3.cloned.1.call-start = ((), (), s32[]{:S(2)}) async-start(), calls=%async_computation | async-start | bytes 524288 | tf_op jit(solution)/shard_map/while/body/eval_jaxpr/psum | solution.py:48
  7.2 21.4 %collective-permute-start = (bf16[128,128]{1,0:T(8,128)(2,1)}, bf16[128,128]{1,0:T(8,128)(2,1)S(1)}, u32[]{:S(2)}, u32[]{:S(2)}) collective-permute-start(bf16[128,128]{1,0:T(8,128)(2,1)} %param.12), channel_id=1, source_target_pairs={{16,0},{0,16},{17,1},{1,17},{18,2},{2,18},{19,3},{3,19},{20,4},{4,... | collective-permute-start | bytes 98312 | tf_op jit(solution)/shard_map/while/body/eval_jaxpr/ppermute | solution.py:13
  10.3 19.8 %collective-permute-start.1 = (bf16[128,576]{0,1:T(8,128)(2,1)}, bf16[128,576]{0,1:T(8,128)(2,1)S(1)}, u32[]{:S(2)}, u32[]{:S(2)}) collective-permute-start(bf16[128,576]{0,1:T(8,128)(2,1)} %param.9), channel_id=1, source_target_pairs={{16,0},{0,16},{17,1},{1,17},{18,2},{2,18},{19,3},{3,19},{20,4},{4,... | collective-permute-start | bytes 442376 | tf_op jit(solution)/shard_map/while/body/eval_jaxpr/ppermute | solution.py:13
  15.7 6.7 %copy-start.4 = (bf16[128,576]{0,1:T(8,128)(2,1)S(1)}, bf16[128,576]{0,1:T(8,128)(2,1)}, u32[]{:S(2)}) copy-start(bf16[128,576]{0,1:T(8,128)(2,1)} %param.9) | copy-start | bytes 442372
  15.7 6.7 %copy-start.5 = (f32[32,128]{1,0:T(8,128)S(1)}, f32[32,128]{1,0:T(8,128)}, u32[]{:S(2)}) copy-start(f32[32,128]{1,0:T(8,128)} %param.10) | copy-start | bytes 49156
  22.4 7.6 %slice-start = ((s8[4718592]{0:T(1024)(128)(4,1)}), s8[4194304]{0:T(1024)(128)(4,1)S(1)}, s32[]{:S(2)}) async-start(s8[4718592]{0:T(1024)(128)(4,1)} %bitcast.89), calls=%async_computation.1 | async-start | bytes 8388608
  22.4 7.6 %slice-start.1 = ((s8[4718592]{0:T(1024)(128)(4,1)}), s8[524288]{0:T(1024)(128)(4,1)S(1)}, s32[]{:S(2)}) async-start(s8[4718592]{0:T(1024)(128)(4,1)} %bitcast.89), calls=%async_computation.2 | async-start | bytes 1048576
  30.0 37.2 %copy-start.3 = (f32[128]{0:T(128)S(1)}, f32[128]{0:T(128)}, u32[]{:S(2)}) copy-start(f32[128]{0:T(128)} %param.14) | copy-start | bytes 1540
  30.0 38.3 %copy-start.2 = (f32[16,128]{1,0:T(8,128)S(1)}, f32[16,128]{1,0:T(8,128)}, u32[]{:S(2)}) copy-start(f32[16,128]{1,0:T(8,128)} %param.13) | copy-start | bytes 24580
  32.9 36.1 %copy-start.1 = (bf16[128,128]{1,0:T(8,128)(2,1)S(1)}, bf16[128,128]{1,0:T(8,128)(2,1)}, u32[]{:S(2)}) copy-start(bf16[128,128]{1,0:T(8,128)(2,1)} %param.12) | copy-start | bytes 98308
  70.0 4.3 %collective-permute-start.2 = (f32[128,128]{1,0:T(8,128)S(1)}, f32[128,128]{1,0:T(8,128)S(1)}, u32[]{:S(2)}, u32[]{:S(2)}) collective-permute-start(f32[128,128]{1,0:T(8,128)S(1)} %convolution_bitcast_fusion.1), channel_id=1, source_target_pairs={{16,0},{0,16},{17,1},{1,17},{18,2},{2,18},{19,3},{3,19},{20,4},{4,... | collective-permute-start | bytes 196616 | tf_op jit(solution)/shard_map/while/body/eval_jaxpr/ppermute | solution.py:13
  75.1 4.3 %collective-permute-start.3 = (f32[128,128]{1,0:T(8,128)S(1)}, f32[128,128]{1,0:T(8,128)S(1)}, u32[]{:S(2)}, u32[]{:S(2)}) collective-permute-start(f32[128,128]{1,0:T(8,128)S(1)} %fusion), channel_id=1, source_target_pairs={{16,0},{0,16},{17,1},{1,17},{18,2},{2,18},{19,3},{3,19},{20,4},{4,... | collective-permute-start | bytes 196616 | tf_op jit(solution)/shard_map/ppermute | solution.py:13
Sparse Core Ops, SparseCore 0:
  33.0 34.1 all-reduce.2
